TPU v7x, 32 devices: a whole 2x2x4 slice. The times are simulated.
32 devices in a mesh: tm: 8 (over z, y), roll: 4 (over x, core).
Axes of the slice: x: 2, y: 2, z: 4, core: 2. Of those that a mesh axis runs over, the one named last changes fastest.
Arguments:
- inputs: bfloat16 [4, 64, 32, 2048], P('roll', 'tm'), may hold values from -30 to 30
- cotangent: bfloat16 [4, 64, 32, 2048], P('roll', 'tm'), may hold values from -6 to 6
- memory_lists: int32 [4, 64, 8], P('roll', 'tm'), may hold values from -1 to 55, as said below
- w_query: bfloat16 [2048, 1024], replicated, may hold values from -1 to 1
- w_key: bfloat16 [2048, 1024], replicated, may hold values from -1 to 1
- w_value: bfloat16 [2048, 1024], replicated, may hold values from -0.125 to 0.125
- w_output: bfloat16 [1024, 2048], replicated, may hold values from -0.1875 to 0.1875
Outputs:
- attended: bfloat16 [4, 64, 32, 2048], P('roll', 'tm')
- grad_input: bfloat16 [4, 64, 32, 2048], P('roll', 'tm')
- grad_w_query: float32 [2048, 1024], P('tm')
- grad_w_key: float32 [2048, 1024], P('tm')
- grad_w_value: float32 [2048, 1024], P('tm')
- grad_w_output: float32 [1024, 2048], P('tm')
Inputs may be any that keep to these rules, and one draw needn't show every extreme that they name: `memory_lists`: every entry is -1 or a frame of the same rollout that lies in an earlier block of 8 frames and before frame f - 4. The frames named in one list differ, and -1 entries come after them. The frames of one block name at most 3 distinct frames of any other block, and exactly 3 of the block just before theirs.
All inputs are finite; a program needn't handle non-finite values.
Results may differ from a plain program's by a relative error of at most 0.02.
Values may be sent and summed in bfloat16 or wider, within the bound.
A program may use at most 192 MiB of HBM per device.

v0:
```python
import jax
import jax.numpy as jnp
from jax import lax
from jax.sharding import PartitionSpec as P

HEADS = 8
HEAD = 128
BAND = 4
MEM = 8
CAP = 3
masked_score = -1e30


def from_behind(block, axis, distance):
    devices = range(lax.axis_size(axis))
    route = [(i - distance, i) for i in devices if i - distance in devices]
    return lax.ppermute(block, axis, route)


def dot_last(left, right):
    return lax.dot_general(
        left, right, (((1,), (1,)), ((), ())), preferred_element_type=jnp.float32
    )


def dot_first(left, right):
    return lax.dot_general(
        left, right, (((0,), (0,)), ((), ())), preferred_element_type=jnp.float32
    )


def attend(queries, key_set, value_set, key_valid, grad_heads):
    frame_count, key_count, frame_tokens, inner_width = key_set.shape
    score_scale = HEAD ** (-0.5)
    query_h = queries.reshape(frame_count, frame_tokens, HEADS, HEAD)
    key_h = key_set.reshape(frame_count, key_count * frame_tokens, HEADS, HEAD)
    value_h = value_set.reshape(frame_count, key_count * frame_tokens, HEADS, HEAD)
    grad_h = grad_heads.reshape(frame_count, frame_tokens, HEADS, HEAD)
    scores = (
        jnp.einsum("fqhe,fkhe->fhqk", query_h, key_h, preferred_element_type=jnp.float32)
        * score_scale
    )
    key_mask = jnp.repeat(key_valid, frame_tokens, axis=1)[:, None, None, :]
    scores = jnp.where(key_mask, scores, masked_score)
    row_max = jnp.max(scores, axis=-1, keepdims=True)
    weights = jnp.exp(scores - row_max)
    weights = weights / jnp.sum(weights, axis=-1, keepdims=True)
    rounded = weights.astype(jnp.bfloat16)
    heads_out = jnp.einsum(
        "fhqk,fkhe->fqhe", rounded, value_h, preferred_element_type=jnp.float32
    ).astype(jnp.bfloat16)
    grad_prob = jnp.einsum("fqhe,fkhe->fhqk", grad_h, value_h, preferred_element_type=jnp.float32)
    row_dot = jnp.sum(weights * grad_prob, axis=-1, keepdims=True)
    dscore = (weights * (grad_prob - row_dot)).astype(jnp.bfloat16)
    grad_query = (
        jnp.einsum("fhqk,fkhe->fqhe", dscore, key_h, preferred_element_type=jnp.float32)
        * score_scale
    ).astype(jnp.bfloat16)
    grad_keys = (
        jnp.einsum("fhqk,fqhe->fkhe", dscore, query_h, preferred_element_type=jnp.float32)
        * score_scale
    )
    grad_values = jnp.einsum("fhqk,fqhe->fkhe", rounded, grad_h, preferred_element_type=jnp.float32)
    block_shape = (frame_count, key_count, frame_tokens, inner_width)
    return (
        heads_out.reshape(frame_count, frame_tokens, inner_width),
        grad_query.reshape(frame_count, frame_tokens, inner_width),
        grad_keys.reshape(block_shape),
        grad_values.reshape(block_shape),
    )


def spread_band(grad_band):
    frame_count, unused, frame_tokens, inner_width = grad_band.shape
    spread = jnp.zeros((frame_count + BAND, frame_tokens, inner_width), jnp.float32)
    for offset in range(BAND + 1):
        spread = spread + jnp.pad(grad_band[:, offset], ((offset, BAND - offset), (0, 0), (0, 0)))
    return spread


def slot_sum(hit_matrix, part):
    flat = part.reshape(part.shape[0] * part.shape[1], -1)
    high = flat.astype(jnp.bfloat16)
    low = (flat - high.astype(jnp.float32)).astype(jnp.bfloat16)
    return dot_first(hit_matrix, high) + dot_first(hit_matrix, low)


def local(inputs, cotangent, memory_lists, w_query, w_key, w_value, w_output):
    frame_count, frame_tokens, model_width = inputs.shape[1:]
    inner_width = w_query.shape[1]
    blocks = lax.axis_size("tm")
    position = lax.axis_index("tm")
    row_count = frame_count * frame_tokens
    flat_input = inputs.reshape(row_count, model_width)
    grad_flat = cotangent.reshape(row_count, model_width)
    queries = jnp.dot(flat_input, w_query, preferred_element_type=jnp.float32).astype(jnp.bfloat16)
    key_rows = jnp.dot(flat_input, w_key, preferred_element_type=jnp.float32).astype(jnp.bfloat16)
    value_rows = jnp.dot(flat_input, w_value, preferred_element_type=jnp.float32).astype(
        jnp.bfloat16
    )
    key_frames = key_rows.reshape(frame_count, frame_tokens, inner_width)
    value_frames = value_rows.reshape(frame_count, frame_tokens, inner_width)
    grad_heads = dot_last(grad_flat, w_output).astype(jnp.bfloat16)
    recalled = memory_lists[0]
    first_frame = position * frame_count
    last_frames = jnp.concatenate(
        [key_frames[frame_count - BAND :], value_frames[frame_count - BAND :]], axis=-1
    )
    before = from_behind(last_frames, "tm", 1)
    extended_keys = jnp.concatenate([before[..., :inner_width], key_frames], axis=0)
    extended_values = jnp.concatenate([before[..., inner_width:], value_frames], axis=0)
    band_keys = jnp.stack(
        [extended_keys[offset : offset + frame_count] for offset in range(BAND + 1)], axis=1
    )
    band_values = jnp.stack(
        [extended_values[offset : offset + frame_count] for offset in range(BAND + 1)], axis=1
    )
    band_index = (
        jnp.arange(frame_count, dtype=jnp.int32)[:, None]
        + jnp.arange(BAND + 1, dtype=jnp.int32)[None, :]
    )
    band_ok = first_frame + band_index - BAND >= 0
    all_lists = lax.all_gather(recalled, "tm", axis=0, tiled=True)
    targets = jnp.arange(blocks * frame_count, dtype=jnp.int32)
    wanted = jnp.any(recalled.reshape(-1, 1) == targets[None, :], axis=0).reshape(
        blocks, frame_count
    )
    slot_rank = jnp.cumsum(wanted.astype(jnp.int32), axis=1) - 1
    slot_table = (jnp.arange(blocks, dtype=jnp.int32)[:, None] * CAP + slot_rank).reshape(-1)
    mem_ok = recalled >= 0
    safe_ids = jnp.where(mem_ok, recalled, 0)
    slot_ids = jnp.where(mem_ok, slot_table[safe_ids], 0)
    own_frames = first_frame + jnp.arange(frame_count, dtype=jnp.int32)
    requested = jnp.any(
        all_lists.reshape(blocks, frame_count * MEM, 1) == own_frames[None, None, :], axis=1
    )
    asked_rank = jnp.cumsum(requested.astype(jnp.int32), axis=1) - 1
    picker = requested[:, None, :] & (
        asked_rank[:, None, :] == jnp.arange(CAP, dtype=jnp.int32)[None, :, None]
    )
    picker = picker.astype(jnp.bfloat16)
    out_keys = jnp.einsum(
        "bcp,pz->bcz", picker, key_rows.reshape(frame_count, -1), preferred_element_type=jnp.float32
    )
    out_values = jnp.einsum(
        "bcp,pz->bcz",
        picker,
        value_rows.reshape(frame_count, -1),
        preferred_element_type=jnp.float32,
    )
    piece_shape = (blocks, CAP, frame_tokens, inner_width)
    outgoing = jnp.concatenate(
        [
            out_keys.astype(jnp.bfloat16).reshape(piece_shape),
            out_values.astype(jnp.bfloat16).reshape(piece_shape),
        ],
        axis=-1,
    )
    incoming = lax.all_to_all(outgoing, "tm", split_axis=0, concat_axis=0, tiled=True)
    slot_rows = incoming.reshape(blocks * CAP, frame_tokens, 2 * inner_width)
    memory_keys = slot_rows[..., :inner_width][slot_ids]
    memory_values = slot_rows[..., inner_width:][slot_ids]
    key_set = jnp.concatenate([band_keys, memory_keys], axis=1)
    value_set = jnp.concatenate([band_values, memory_values], axis=1)
    key_valid = jnp.concatenate([band_ok, mem_ok], axis=1)
    heads_out, grad_query, grad_keys_all, grad_values_all = attend(
        queries.reshape(frame_count, frame_tokens, inner_width),
        key_set,
        value_set,
        key_valid,
        grad_heads.reshape(frame_count, frame_tokens, inner_width),
    )
    key_spread = spread_band(grad_keys_all[:, : BAND + 1])
    value_spread = spread_band(grad_values_all[:, : BAND + 1])
    rim = jnp.concatenate([key_spread[:BAND], value_spread[:BAND]], axis=-1).astype(jnp.bfloat16)
    passed = from_behind(rim, "tm", -1)
    passed_full = jnp.pad(passed.astype(jnp.float32), ((frame_count - BAND, 0), (0, 0), (0, 0)))
    slot_hits = (
        slot_ids.reshape(-1, 1) == jnp.arange(blocks * CAP, dtype=jnp.int32)[None, :]
    ) & mem_ok.reshape(-1, 1)
    hit_matrix = slot_hits.astype(jnp.bfloat16)
    slot_keys = (
        slot_sum(hit_matrix, grad_keys_all[:, BAND + 1 :]).astype(jnp.bfloat16).reshape(piece_shape)
    )
    slot_values = (
        slot_sum(hit_matrix, grad_values_all[:, BAND + 1 :])
        .astype(jnp.bfloat16)
        .reshape(piece_shape)
    )
    slot_grad = jnp.concatenate([slot_keys, slot_values], axis=-1)
    returned = lax.all_to_all(slot_grad, "tm", split_axis=0, concat_axis=0, tiled=True)
    gathered_back = jnp.einsum(
        "bcp,bcz->pz", picker, returned.reshape(blocks, CAP, -1), preferred_element_type=jnp.float32
    )
    gathered_back = gathered_back.reshape(frame_count, frame_tokens, 2 * inner_width)
    grad_keys = (
        key_spread[BAND:] + passed_full[..., :inner_width] + gathered_back[..., :inner_width]
    ).astype(jnp.bfloat16)
    grad_values = (
        value_spread[BAND:] + passed_full[..., inner_width:] + gathered_back[..., inner_width:]
    ).astype(jnp.bfloat16)
    grad_keys = grad_keys.reshape(row_count, inner_width)
    grad_values = grad_values.reshape(row_count, inner_width)
    query_rows = grad_query.reshape(row_count, inner_width)
    heads_rows = heads_out.reshape(row_count, inner_width)
    grad_input = (
        dot_last(query_rows, w_query) + dot_last(grad_keys, w_key) + dot_last(grad_values, w_value)
    )
    grad_input = grad_input.astype(jnp.bfloat16).reshape(1, frame_count, frame_tokens, model_width)
    attended = jnp.dot(heads_rows, w_output, preferred_element_type=jnp.float32).astype(
        jnp.bfloat16
    )
    attended = attended.reshape(1, frame_count, frame_tokens, model_width)
    partials = (
        dot_first(flat_input, query_rows).astype(jnp.bfloat16),
        dot_first(flat_input, grad_keys).astype(jnp.bfloat16),
        dot_first(flat_input, grad_values).astype(jnp.bfloat16),
        dot_first(heads_rows, grad_flat).astype(jnp.bfloat16),
    )
    shares = (
        lax.psum_scatter(partials[0], "tm", scatter_dimension=0, tiled=True).astype(jnp.float32),
        lax.psum_scatter(partials[1], "tm", scatter_dimension=0, tiled=True).astype(jnp.float32),
        lax.psum_scatter(partials[2], "tm", scatter_dimension=0, tiled=True).astype(jnp.float32),
        lax.psum_scatter(partials[3], "tm", scatter_dimension=0, tiled=True).astype(jnp.float32),
    )
    totals = (
        lax.psum(shares[0].astype(jnp.bfloat16), "roll").astype(jnp.float32),
        lax.psum(shares[1].astype(jnp.bfloat16), "roll").astype(jnp.float32),
        lax.psum(shares[2].astype(jnp.bfloat16), "roll").astype(jnp.float32),
        lax.psum(shares[3].astype(jnp.bfloat16), "roll").astype(jnp.float32),
    )
    return (attended, grad_input, totals[0], totals[1], totals[2], totals[3])


def solution(mesh):
    return jax.shard_map(
        local,
        mesh=mesh,
        in_specs=(
            P("roll", "tm", None, None),
            P("roll", "tm", None, None),
            P("roll", "tm", None),
            P(),
            P(),
            P(),
            P(),
        ),
        out_specs=(
            P("roll", "tm", None, None),
            P("roll", "tm", None, None),
            P("tm", None),
            P("tm", None),
            P("tm", None),
            P("tm", None),
        ),
        check_vma=False,
    )
```

profile of v0, /device:TPU:0, one launch (start us, length us, event | category | flops | bytes accessed | tf_op | source)
XLA Modules:
  0.0 683.3 jit_solution(1070487191711943485)
XLA Ops:
  7.2 32.7 %all-gather = s32[1,64,8]{2,1,0:T(8,128)S(1)} all-gather(s32[1,8,8]{2,1,0:T(8,128)} %param.9), channel_id=2, replica_groups=mesh['tm'=8,'roll'=4] {'tm'}, dimensions={1}, use_global_device_ids=true | all-gather | bytes 2304 | tf_op jit(solution)/shard_map/all_gather | solution.py:123
  40.6 3.6 convolution_convert_fusion.6
  50.9 5.6 all-to-all-start
  57.5 4.8 collective-permute-start
  70.2 19.8 %collective-permute-done = bf16[4,32,2048]{2,1,0:T(8,128)(2,1)} collective-permute-done((bf16[4,32,2048]{2,1,0:T(8,128)(2,1)}, bf16[4,32,2048]{2,1,0:T(8,128)(2,1)}, u32[]{:S(2)}, u32[]{:S(2)}) %collective-permute-start) | collective-permute-done | bytes 524320 | tf_op jit(solution)/shard_map/ppermute | solution.py:17
  99.3 21.9 %all-to-all-done = bf16[8,3,32,2048]{3,2,1,0:T(8,128)(2,1)} async-done(((bf16[8,3,32,2048]{3,2,1,0:T(8,128)(2,1)}), bf16[8,3,32,2048]{3,2,1,0:T(8,128)(2,1)}, u32[]{:S(2)}, u32[]{:S(2)}) %all-to-all-start) | async-done | bytes 3145760 | tf_op jit(solution)/shard_map/all_to_all | solution.py:159
  124.7 4.2 gather_fusion.2
  131.7 5.0 constant_dynamic-update-slice_fusion.2
  136.7 4.9 copy.180
  144.4 5.5 copy.179
  155.1 4.5 multiply_reduce_fusion
  168.1 5.8 fusion.42
  174.9 7.0 %convolution_bitcast_fusion = f32[8,416,8,128]{3,1,2,0:T(8,128)} fusion(bf16[8,32,8,128]{3,2,1,0:T(8,128)(2,1)S(1)} %bitcast.264, f32[8,8,32,416]{3,2,1,0:T(8,128)S(1)} %copy-done.3, f32[8,8,32]{2,1,0:T(8,128)S(1)} %get-tuple-element.50), kind=kOutput, calls=%fused_computation.15 | convolution fusion | flops 219807744 | bytes 17571840 | tf_op jit(solution)/shard_map/fhqk,fqhe->fkhe/dot_general | solution.py:63
  181.9 17.5 %copy.151 = f32[8,416,8,128]{3,2,1,0:T(8,128)} copy(f32[8,416,8,128]{3,1,2,0:T(8,128)} %convolution_bitcast_fusion) | data formatting | bytes 27262976 | tf_op jit(solution)/shard_map/fhqk,fqhe->fkhe/transpose | solution.py:63
  199.4 15.8 %reshape.193 = f32[8,13,32,1024]{3,2,1,0:T(8,128)} reshape(f32[8,416,8,128]{3,2,1,0:T(8,128)} %copy.151) | data formatting | bytes 27262976 | tf_op jit(solution)/shard_map/reshape | solution.py:69
  215.1 4.3 slice_bitcast_fusion
  219.4 5.0 copy.186
  228.3 6.3 multiply_bitcast_fusion
  234.6 17.5 %copy.144 = f32[8,416,8,128]{3,2,1,0:T(8,128)} copy(f32[8,416,8,128]{3,1,2,0:T(8,128)} %multiply_bitcast_fusion) | data formatting | bytes 27262976 | tf_op jit(solution)/shard_map/mul | solution.py:60
  252.1 16.0 %reshape.192 = f32[8,13,32,1024]{3,2,1,0:T(8,128)} reshape(f32[8,416,8,128]{3,2,1,0:T(8,128)} %copy.144) | data formatting | bytes 27262976 | tf_op jit(solution)/shard_map/reshape | solution.py:68
  271.6 4.3 slice_bitcast_fusion.1
  275.9 5.0 copy.184
  286.1 23.4 %all-to-all-start.1 = ((bf16[8,3,32,2048]{3,2,1,0:T(8,128)(2,1)}), bf16[8,3,32,2048]{3,2,1,0:T(8,128)(2,1)}, u32[]{:S(2)}, u32[]{:S(2)}) async-start(bf16[8,3,32,2048]{3,2,1,0:T(8,128)(2,1)} %pad_maximum_fusion.1), calls=%async_computation.1 | async-start | bytes 6291456 | tf_op jit(solution)/shard_map/all_to_all | solution.py:191
  327.6 21.7 %collective-permute-done.1 = bf16[4,32,2048]{2,0,1:T(4,128)(2,1)S(1)} collective-permute-done((bf16[4,32,2048]{2,0,1:T(4,128)(2,1)S(1)}, bf16[4,32,2048]{2,0,1:T(4,128)(2,1)S(1)}, u32[]{:S(2)}, u32[]{:S(2)}) %collective-permute-start.1) | collective-permute-done | bytes 524320 | tf_op jit(solution)/shard_map/ppermute | solution.py:17
  349.6 52.4 %all-to-all-done.1 = bf16[8,3,32,2048]{3,2,1,0:T(8,128)(2,1)} async-done(((bf16[8,3,32,2048]{3,2,1,0:T(8,128)(2,1)}), bf16[8,3,32,2048]{3,2,1,0:T(8,128)(2,1)}, u32[]{:S(2)}, u32[]{:S(2)}) %all-to-all-start.1) | async-done | bytes 3145760 | tf_op jit(solution)/shard_map/all_to_all | solution.py:191
  402.0 4.0 copy.157
  406.0 5.2 reshape.198
  423.5 4.5 convolution_convert_fusion.3
  431.0 92.4 %reduce-scatter.9.cloned.1.call-done = bf16[256,1024]{0,1:T(8,128)(2,1)} async-done(((bf16[2048,1024]{0,1:T(8,128)(2,1)}), bf16[256,1024]{0,1:T(8,128)(2,1)}) %reduce-scatter.9.cloned.1.call-update) | async-done | bytes 524304 | tf_op jit(solution)/shard_map/reduce_scatter | solution.py:223
  523.4 91.8 %reduce-scatter.7.cloned.1.call-done = bf16[256,1024]{0,1:T(8,128)(2,1)} async-done(((bf16[2048,1024]{0,1:T(8,128)(2,1)}), bf16[256,1024]{0,1:T(8,128)(2,1)}) %reduce-scatter.7.cloned.1.call-update) | async-done | bytes 524304 | tf_op jit(solution)/shard_map/reduce_scatter | solution.py:222
  615.3 3.6 fusion.68
  623.4 45.4 %all-reduce.14.cloned.1.call-done = (bf16[256,1024]{0,1:T(8,128)(2,1)}, bf16[256,1024]{0,1:T(8,128)(2,1)}, bf16[256,1024]{0,1:T(8,128)(2,1)}, bf16[128,2048]{1,0:T(8,128)(2,1)}) async-done(((bf16[256,1024]{0,1:T(8,128)(2,1)}, bf16[256,1024]{0,1:T(8,128)(2,1)}, bf16[256,1024]{0,1:T(8,128)(2,1)}, bf16[128,2048]{1,0:T(8,128)(2,1)}), (bf16[256,1024]{0,1:T(8,128)(2,1)}, bf16[256,1024]{0,1:T(8,128)(2,1)}, ...) | async-done | bytes 2097168 | tf_op jit(solution)/shard_map/psum | solution.py:227
  (179 shorter events, 107.1 us)
Async XLA Ops:
  7.2 33.4 %copy-start = (bf16[1,8,32,2048]{3,2,1,0:T(8,128)(2,1)S(1)}, bf16[1,8,32,2048]{3,2,1,0:T(8,128)(2,1)}, u32[]{:S(2)}) copy-start(bf16[1,8,32,2048]{3,2,1,0:T(8,128)(2,1)} %param.7) | copy-start | bytes 3145732
  40.3 7.2 %copy-start.27 = (pred[8,8]{0,1:T(8,128)(4,1)}, pred[8,8]{0,1:T(8,128)(4,1)S(1)}, u32[]{:S(2)}) copy-start(pred[8,8]{0,1:T(8,128)(4,1)S(1)} %copy.121) | copy-start | bytes 196
  40.6 6.9 %copy-start.25 = (s32[8,8]{0,1:T(8,128)}, s32[8,8]{0,1:T(8,128)S(1)}, u32[]{:S(2)}) copy-start(s32[8,8]{0,1:T(8,128)S(1)} %copy.122) | copy-start | bytes 772
  40.6 3.6 copy-start.12
  50.9 11.4 %copy-start.24 = (s32[1,8,8]{2,1,0:T(8,128)S(1)}, s32[1,8,8]{2,1,0:T(8,128)}, u32[]{:S(2)}) copy-start(s32[1,8,8]{2,1,0:T(8,128)} %param.9) | copy-start | bytes 772
  50.9 70.3 %all-to-all-start = ((bf16[8,3,32,2048]{3,2,1,0:T(8,128)(2,1)}), bf16[8,3,32,2048]{3,2,1,0:T(8,128)(2,1)}, u32[]{:S(2)}, u32[]{:S(2)}) async-start(bf16[8,3,32,2048]{3,2,1,0:T(8,128)(2,1)} %pad_maximum_fusion), calls=%async_computation | async-start | bytes 6291456 | tf_op jit(solution)/shard_map/all_to_all | solution.py:159
  56.6 371.5 %reduce-scatter.5.cloned.1.call-start = ((), (), s32[]{:S(2)}) async-start(), calls=%async_computation.6 | async-start | bytes 4718592 | tf_op jit(solution)/shard_map/reduce_scatter | solution.py:221
  57.5 32.6 %collective-permute-start = (bf16[4,32,2048]{2,1,0:T(8,128)(2,1)}, bf16[4,32,2048]{2,1,0:T(8,128)(2,1)}, u32[]{:S(2)}, u32[]{:S(2)}) collective-permute-start(bf16[4,32,2048]{2,1,0:T(8,128)(2,1)} %pad_maximum_fusion.4), channel_id=1, source_target_pairs={{0,4},{4,8},{8,12},{12,16},{16,20},{20,24},{24,28},{1,5},{5,9},{9,... | collective-permute-start | bytes 1572872 | tf_op jit(solution)/shard_map/ppermute | solution.py:17
  64.3 3.7 copy-start.21
  64.3 3.8 copy-start.29
  68.0 81.9 %copy-start.10 = (bf16[32,8,8,128]{3,2,1,0:T(8,128)(2,1)}, bf16[32,8,8,128]{3,2,1,0:T(8,128)(2,1)S(1)}, u32[]{:S(2)}) copy-start(bf16[32,8,8,128]{3,2,1,0:T(8,128)(2,1)S(1)} %copy.178) | copy-start | bytes 1572868
  136.7 4.9 copy-start.1
  141.6 13.5 %copy-start.4 = (bf16[416,8,8,128]{3,2,1,0:T(8,128)(2,1)}, bf16[416,8,8,128]{3,2,1,0:T(8,128)(2,1)S(1)}, u32[]{:S(2)}) copy-start(bf16[416,8,8,128]{3,2,1,0:T(8,128)(2,1)S(1)} %copy.180) | copy-start | bytes 20447236
  155.1 4.6 copy-start.2
  168.0 263.0 %reduce-scatter.11.cloned.1.call-start = ((), (), s32[]{:S(2)}) async-start(), calls=%async_computation.9 | async-start | bytes 4718592 | tf_op jit(solution)/shard_map/reduce_scatter | solution.py:224
  168.0 6.9 %copy-start.3 = (f32[8,8,32,416]{3,2,1,0:T(8,128)S(1)}, f32[8,8,32,416]{3,2,1,0:T(8,128)}, u32[]{:S(2)}) copy-start(f32[8,8,32,416]{3,2,1,0:T(8,128)} %copy-done.2) | copy-start | bytes 10223620
  168.1 6.9 %copy-start.20 = (bf16[32,8,8,128]{3,2,1,0:T(8,128)(2,1)S(1)}, bf16[32,8,8,128]{3,2,1,0:T(8,128)(2,1)}, u32[]{:S(2)}) copy-start(bf16[32,8,8,128]{3,2,1,0:T(8,128)(2,1)} %copy.182) | copy-start | bytes 1572868
  252.1 16.1 %copy-start.16 = (bf16[8,32,8,128]{3,2,1,0:T(8,128)(2,1)S(1)}, bf16[8,32,8,128]{3,2,1,0:T(8,128)(2,1)}, u32[]{:S(2)}) copy-start(bf16[8,32,8,128]{3,2,1,0:T(8,128)(2,1)} %copy.138) | copy-start | bytes 1572868
  252.1 16.1 %copy-start.22 = (bf16[1,8,32,2048]{3,2,1,0:T(8,128)(2,1)S(1)}, bf16[1,8,32,2048]{3,2,1,0:T(8,128)(2,1)}, u32[]{:S(2)}) copy-start(bf16[1,8,32,2048]{3,2,1,0:T(8,128)(2,1)} %param.8) | copy-start | bytes 3145732
  286.1 115.9 %all-to-all-start.1 = ((bf16[8,3,32,2048]{3,2,1,0:T(8,128)(2,1)}), bf16[8,3,32,2048]{3,2,1,0:T(8,128)(2,1)}, u32[]{:S(2)}, u32[]{:S(2)}) async-start(bf16[8,3,32,2048]{3,2,1,0:T(8,128)(2,1)} %pad_maximum_fusion.1), calls=%async_computation.1 | async-start | bytes 6291456 | tf_op jit(solution)/shard_map/all_to_all | solution.py:191
  309.5 214.0 %reduce-scatter.9.cloned.1.call-start = ((), (), s32[]{:S(2)}) async-start(), calls=%async_computation.8 | async-start | bytes 4718592 | tf_op jit(solution)/shard_map/reduce_scatter | solution.py:223
  326.1 23.2 %collective-permute-start.1 = (bf16[4,32,2048]{2,0,1:T(4,128)(2,1)S(1)}, bf16[4,32,2048]{2,0,1:T(4,128)(2,1)S(1)}, u32[]{:S(2)}, u32[]{:S(2)}) collective-permute-start(bf16[4,32,2048]{2,0,1:T(4,128)(2,1)S(1)} %pad_maximum_fusion.5), channel_id=1, source_target_pairs={{4,0},{8,4},{12,8},{16,12},{20,16},{24,20},{28,24},{5,1},{9,5},{13... | collective-permute-start | bytes 1572872 | tf_op jit(solution)/shard_map/ppermute | solution.py:17
  406.0 5.2 copy-start.26
  406.0 5.2 copy-start.28
  411.2 3.2 copy-start.9
  416.5 3.3 copy-start.18
  419.7 195.5 %reduce-scatter.7.cloned.1.call-start = ((), (), s32[]{:S(2)}) async-start(), calls=%async_computation.7 | async-start | bytes 4718592 | tf_op jit(solution)/shard_map/reduce_scatter | solution.py:222
  420.1 3.4 copy-start.17
  423.4 191.9 %copy-start.15 = (bf16[8,32,8,128]{3,2,1,0:T(8,128)(2,1)S(1)}, bf16[8,32,8,128]{3,2,1,0:T(8,128)(2,1)}, u32[]{:S(2)}) copy-start(bf16[8,32,8,128]{3,2,1,0:T(8,128)(2,1)} %copy-done.14) | copy-start | bytes 1572868
  423.4 245.3 %all-reduce.14.cloned.1.call-start = ((), (), s32[]{:S(2)}) async-start(), calls=%async_computation.10 | async-start | bytes 4194304 | tf_op jit(solution)/shard_map/psum | solution.py:227
  615.3 3.7 copy-start.13
  668.8 6.7 copy-start.23
  (8 other events, 15.8 us)
Sparse Core Ops, SparseCore 0:
  168.1 107.1 reduce-scatter.4
  278.9 152.0 reduce-scatter.10
  434.6 88.7 reduce-scatter.8
  526.9 88.3 reduce-scatter.6
  617.7 51.0 all-reduce.13
where the time goes:
time: 690 us; the launch traced here: 683 us
  waiting for transfers between devices  348 us (50%)
  local copies, waits for them, and re-layouts  159 us (23%)
  matrix products  69.8 us (10%)
  starting transfers between devices  35.7 us (5%)
  blocking collectives  32.7 us (5%)
  other arithmetic  22.6 us (3%)
  between operations  14.8 us (2%)
    reduce_scatter x1, waiting for transfers between devices, local(): lax.psum_scatter(partials[2], 'tm', scatter_dimension=0, tiled=True)  92.4 us
    reduce_scatter x1, waiting for transfers between devices, local(): lax.psum_scatter(partials[1], 'tm', scatter_dimension=0, tiled=True)  91.8 us
    all_to_all x1, waiting for transfers between devices, local(): lax.all_to_all(slot_grad, 'tm', split_axis=0, concat_axis=0, tiled=True)  52.4 us
    unnamed x87, local copies, waits for them, and re-layouts  51.6 us
    psum x1, waiting for transfers between devices, local(): lax.psum(shares[0].astype(jnp.bfloat16), 'roll').astype(jnp.float32)  45.4 us
    ppermute x2, waiting for transfers between devices, from_behind(): return lax.ppermute(block, axis, route)  41.5 us
    all_gather x1, blocking collectives, local(): all_lists = lax.all_gather(recalled, 'tm', axis=0, tiled=True)  32.7 us
    all_to_all x1, starting transfers between devices, local(): lax.all_to_all(slot_grad, 'tm', split_axis=0, concat_axis=0, tiled=True)  23.4 us
  transfers between devices with their start and end apart: 9, of which 8 were waited for; matrix products, arithmetic and copies ran while one was open for 27% of the time, Pallas kernels for 0%

commit v1 on v0

--- a/solution.py
+++ b/solution.py
@@ -9,6 +9,12 @@
 MEM = 8
 CAP = 3
 masked_score = -1e30
+
+
+def summed_here(value, axis):
+    parts = lax.all_gather(value, axis, axis=0, tiled=False)
+    total = parts.sum(axis=0)
+    return total
 
 
 def from_behind(block, axis, distance):
@@ -224,7 +230,7 @@
         lax.psum_scatter(partials[3], "tm", scatter_dimension=0, tiled=True).astype(jnp.float32),
     )
     totals = (
-        lax.psum(shares[0].astype(jnp.bfloat16), "roll").astype(jnp.float32),
+        summed_here(shares[0].astype(jnp.bfloat16), "roll").astype(jnp.float32),
         lax.psum(shares[1].astype(jnp.bfloat16), "roll").astype(jnp.float32),
         lax.psum(shares[2].astype(jnp.bfloat16), "roll").astype(jnp.float32),
         lax.psum(shares[3].astype(jnp.bfloat16), "roll").astype(jnp.float32),

time: 690 us -> 704 us (1.020)
    all_gather x0 -> x1, waiting for transfers between devices: none -> 17.3 us  [summed_here(): parts = lax.all_gather(value, axis, axis=0, tiled=False)]
    psum x1, waiting for transfers between devices: 45.4 us -> 36.1 us  [local(): lax.psum(shares[1].astype(jnp.bfloat16), 'roll').astype(jnp.float32)]
    unnamed x87 -> x85, local copies, waits for them, and re-layouts: 51.6 us -> 50.9 us
  transfers between devices with their start and end apart: 9 -> 10, of which waited for: 8 -> 8; matrix products, arithmetic and copies ran while one was open for 27% -> 28% of each run, Pallas kernels for 0% -> 0%
where the time goes in v1:
time: 704 us; the launch traced here: 698 us
  waiting for transfers between devices  353 us (50%)
  local copies, waits for them, and re-layouts  162 us (23%)
  matrix products  71.9 us (10%)
  starting transfers between devices  35.7 us (5%)
  blocking collectives  32.7 us (5%)
  other arithmetic  27.1 us (4%)
  between operations  15.1 us (2%)
    reduce_scatter x1, waiting for transfers between devices, local(): lax.psum_scatter(partials[1], 'tm', scatter_dimension=0, tiled=True)  91.9 us
    reduce_scatter x1, waiting for transfers between devices, local(): lax.psum_scatter(partials[2], 'tm', scatter_dimension=0, tiled=True)  91.7 us
    all_to_all x1, waiting for transfers between devices, local(): lax.all_to_all(slot_grad, 'tm', split_axis=0, concat_axis=0, tiled=True)  52.4 us
    unnamed x85, local copies, waits for them, and re-layouts  50.9 us
    ppermute x2, waiting for transfers between devices, from_behind(): return lax.ppermute(block, axis, route)  41.4 us
    psum x1, waiting for transfers between devices, local(): lax.psum(shares[1].astype(jnp.bfloat16), 'roll').astype(jnp.float32)  36.1 us
    all_gather x1, blocking collectives, local(): all_lists = lax.all_gather(recalled, 'tm', axis=0, tiled=True)  32.7 us
    all_to_all x1, starting transfers between devices, local(): lax.all_to_all(slot_grad, 'tm', split_axis=0, concat_axis=0, tiled=True)  23.1 us
  transfers between devices with their start and end apart: 10, of which 8 were waited for; matrix products, arithmetic and copies ran while one was open for 28% of the time, Pallas kernels for 0%

profile of v1, /device:TPU:0, one launch (start us, length us, event | category | flops | bytes accessed | tf_op | source)
XLA Modules:
  0.0 697.9 jit_solution(13933031880876175388)
XLA Ops:
  7.2 32.7 %all-gather = s32[1,64,8]{2,1,0:T(8,128)S(1)} all-gather(s32[1,8,8]{2,1,0:T(8,128)} %param.9), channel_id=2, replica_groups=mesh['tm'=8,'roll'=4] {'tm'}, dimensions={1}, use_global_device_ids=true | all-gather | bytes 2304 | tf_op jit(solution)/shard_map/all_gather | solution.py:129
  50.9 5.6 all-to-all-start
  57.5 4.8 collective-permute-start
  70.3 19.8 %collective-permute-done = bf16[4,32,2048]{2,1,0:T(8,128)(2,1)} collective-permute-done((bf16[4,32,2048]{2,1,0:T(8,128)(2,1)}, bf16[4,32,2048]{2,1,0:T(8,128)(2,1)}, u32[]{:S(2)}, u32[]{:S(2)}) %collective-permute-start) | collective-permute-done | bytes 524320 | tf_op jit(solution)/shard_map/ppermute | solution.py:23
  99.1 22.1 %all-to-all-done = bf16[8,3,32,2048]{3,2,1,0:T(8,128)(2,1)} async-done(((bf16[8,3,32,2048]{3,2,1,0:T(8,128)(2,1)}), bf16[8,3,32,2048]{3,2,1,0:T(8,128)(2,1)}, u32[]{:S(2)}, u32[]{:S(2)}) %all-to-all-start) | async-done | bytes 3145760 | tf_op jit(solution)/shard_map/all_to_all | solution.py:165
  124.7 4.2 gather_fusion.2
  131.7 4.9 constant_dynamic-update-slice_fusion.2
  136.7 4.9 copy.178
  144.3 5.5 copy.177
  155.1 4.5 multiply_reduce_fusion
  168.1 5.8 fusion.42
  174.9 7.0 convolution_bitcast_fusion
  181.9 17.5 %copy.149 = f32[8,416,8,128]{3,2,1,0:T(8,128)} copy(f32[8,416,8,128]{3,1,2,0:T(8,128)} %convolution_bitcast_fusion) | data formatting | bytes 27262976 | tf_op jit(solution)/shard_map/fhqk,fqhe->fkhe/transpose | solution.py:69
  199.4 15.8 %reshape.193 = f32[8,13,32,1024]{3,2,1,0:T(8,128)} reshape(f32[8,416,8,128]{3,2,1,0:T(8,128)} %copy.149) | data formatting | bytes 27262976 | tf_op jit(solution)/shard_map/reshape | solution.py:75
  215.2 4.3 slice_bitcast_fusion
  219.4 5.0 copy.184
  228.3 6.3 multiply_bitcast_fusion
  234.6 17.5 %copy.142 = f32[8,416,8,128]{3,2,1,0:T(8,128)} copy(f32[8,416,8,128]{3,1,2,0:T(8,128)} %multiply_bitcast_fusion) | data formatting | bytes 27262976 | tf_op jit(solution)/shard_map/mul | solution.py:66
  252.2 16.0 %reshape.192 = f32[8,13,32,1024]{3,2,1,0:T(8,128)} reshape(f32[8,416,8,128]{3,2,1,0:T(8,128)} %copy.142) | data formatting | bytes 27262976 | tf_op jit(solution)/shard_map/reshape | solution.py:74
  271.6 4.3 slice_bitcast_fusion.1
  275.9 5.0 copy.182
  286.2 23.1 %all-to-all-start.1 = ((bf16[8,3,32,2048]{3,2,1,0:T(8,128)(2,1)}), bf16[8,3,32,2048]{3,2,1,0:T(8,128)(2,1)}, u32[]{:S(2)}, u32[]{:S(2)}) async-start(bf16[8,3,32,2048]{3,2,1,0:T(8,128)(2,1)} %pad_maximum_fusion.1), calls=%async_computation.1 | async-start | bytes 6291456 | tf_op jit(solution)/shard_map/all_to_all | solution.py:197
  327.4 21.7 %collective-permute-done.1 = bf16[4,32,2048]{2,0,1:T(4,128)(2,1)S(1)} collective-permute-done((bf16[4,32,2048]{2,0,1:T(4,128)(2,1)S(1)}, bf16[4,32,2048]{2,0,1:T(4,128)(2,1)S(1)}, u32[]{:S(2)}, u32[]{:S(2)}) %collective-permute-start.1) | collective-permute-done | bytes 524320 | tf_op jit(solution)/shard_map/ppermute | solution.py:23
  349.4 52.4 %all-to-all-done.1 = bf16[8,3,32,2048]{3,2,1,0:T(8,128)(2,1)} async-done(((bf16[8,3,32,2048]{3,2,1,0:T(8,128)(2,1)}), bf16[8,3,32,2048]{3,2,1,0:T(8,128)(2,1)}, u32[]{:S(2)}, u32[]{:S(2)}) %all-to-all-start.1) | async-done | bytes 3145760 | tf_op jit(solution)/shard_map/all_to_all | solution.py:197
  401.8 4.0 copy.155
  405.8 5.2 reshape.198
  424.2 4.6 convolution_convert_fusion.3
  431.5 91.7 %reduce-scatter.9.cloned.1.call-done = bf16[256,1024]{0,1:T(8,128)(2,1)} async-done(((bf16[2048,1024]{0,1:T(8,128)(2,1)}), bf16[256,1024]{0,1:T(8,128)(2,1)}) %reduce-scatter.9.cloned.1.call-update) | async-done | bytes 524304 | tf_op jit(solution)/shard_map/reduce_scatter | solution.py:229
  523.1 91.9 %reduce-scatter.7.cloned.1.call-done = bf16[256,1024]{0,1:T(8,128)(2,1)} async-done(((bf16[2048,1024]{0,1:T(8,128)(2,1)}), bf16[256,1024]{0,1:T(8,128)(2,1)}) %reduce-scatter.7.cloned.1.call-update) | async-done | bytes 524304 | tf_op jit(solution)/shard_map/reduce_scatter | solution.py:228
  615.0 4.3 convolution_add_fusion.3
  621.6 17.3 %all-gather.4.cloned.1.call-done = bf16[1024,1024]{0,1:T(8,128)(2,1)} async-done(((bf16[256,1024]{0,1:T(8,128)(2,1)}), bf16[1024,1024]{0,1:T(8,128)(2,1)}) %all-gather.4.cloned.1.call-update) | async-done | bytes 2097168 | tf_op jit(solution)/shard_map/all_gather | solution.py:15
  648.1 36.1 %all-reduce.14.cloned.1.call-done = (bf16[256,1024]{0,1:T(8,128)(2,1)}, bf16[256,1024]{0,1:T(8,128)(2,1)}, bf16[128,2048]{1,0:T(8,128)(2,1)}) async-done(((bf16[256,1024]{0,1:T(8,128)(2,1)}, bf16[256,1024]{0,1:T(8,128)(2,1)}, bf16[128,2048]{1,0:T(8,128)(2,1)}), (bf16[256,1024]{0,1:T(8,128)(2,1)}, bf16[256,1024]{0,1:T(8,128)(2,1)}, bf16[128,2048]{1,0:T(8,128)(2,1)})) %all-reduce.14.cloned.1.call-update) | async-done | bytes 1572880 | tf_op jit(solution)/shard_map/psum | solution.py:234
  (182 shorter events, 116.8 us)
Async XLA Ops:
  7.2 33.4 %copy-start = (bf16[1,8,32,2048]{3,2,1,0:T(8,128)(2,1)S(1)}, bf16[1,8,32,2048]{3,2,1,0:T(8,128)(2,1)}, u32[]{:S(2)}) copy-start(bf16[1,8,32,2048]{3,2,1,0:T(8,128)(2,1)} %param.7) | copy-start | bytes 3145732
  40.3 7.2 %copy-start.25 = (pred[8,8]{0,1:T(8,128)(4,1)}, pred[8,8]{0,1:T(8,128)(4,1)S(1)}, u32[]{:S(2)}) copy-start(pred[8,8]{0,1:T(8,128)(4,1)S(1)} %copy.119) | copy-start | bytes 196
  40.6 6.9 copy-start.23
  40.6 3.6 copy-start.12
  50.9 11.4 %copy-start.22 = (s32[1,8,8]{2,1,0:T(8,128)S(1)}, s32[1,8,8]{2,1,0:T(8,128)}, u32[]{:S(2)}) copy-start(s32[1,8,8]{2,1,0:T(8,128)} %param.9) | copy-start | bytes 772
  50.9 70.3 %all-to-all-start = ((bf16[8,3,32,2048]{3,2,1,0:T(8,128)(2,1)}), bf16[8,3,32,2048]{3,2,1,0:T(8,128)(2,1)}, u32[]{:S(2)}, u32[]{:S(2)}) async-start(bf16[8,3,32,2048]{3,2,1,0:T(8,128)(2,1)} %pad_maximum_fusion), calls=%async_computation | async-start | bytes 6291456 | tf_op jit(solution)/shard_map/all_to_all | solution.py:165
  56.6 366.7 %reduce-scatter.5.cloned.1.call-start = ((), (), s32[]{:S(2)}) async-start(), calls=%async_computation.6 | async-start | bytes 4718592 | tf_op jit(solution)/shard_map/reduce_scatter | solution.py:227
  57.5 32.6 %collective-permute-start = (bf16[4,32,2048]{2,1,0:T(8,128)(2,1)}, bf16[4,32,2048]{2,1,0:T(8,128)(2,1)}, u32[]{:S(2)}, u32[]{:S(2)}) collective-permute-start(bf16[4,32,2048]{2,1,0:T(8,128)(2,1)} %pad_maximum_fusion.4), channel_id=1, source_target_pairs={{0,4},{4,8},{8,12},{12,16},{16,20},{20,24},{24,28},{1,5},{5,9},{9,... | collective-permute-start | bytes 1572872 | tf_op jit(solution)/shard_map/ppermute | solution.py:23
  64.3 3.7 copy-start.20
  64.3 3.8 copy-start.27
  68.0 81.9 %copy-start.10 = (bf16[32,8,8,128]{3,2,1,0:T(8,128)(2,1)}, bf16[32,8,8,128]{3,2,1,0:T(8,128)(2,1)S(1)}, u32[]{:S(2)}) copy-start(bf16[32,8,8,128]{3,2,1,0:T(8,128)(2,1)S(1)} %copy.176) | copy-start | bytes 1572868
  136.7 4.9 copy-start.1
  141.6 13.5 %copy-start.4 = (bf16[416,8,8,128]{3,2,1,0:T(8,128)(2,1)}, bf16[416,8,8,128]{3,2,1,0:T(8,128)(2,1)S(1)}, u32[]{:S(2)}) copy-start(bf16[416,8,8,128]{3,2,1,0:T(8,128)(2,1)S(1)} %copy.178) | copy-start | bytes 20447236
  155.1 4.6 copy-start.2
  168.0 263.5 %reduce-scatter.11.cloned.1.call-start = ((), (), s32[]{:S(2)}) async-start(), calls=%async_computation.9 | async-start | bytes 4718592 | tf_op jit(solution)/shard_map/reduce_scatter | solution.py:230
  168.0 6.9 copy-start.3
  168.1 6.9 copy-start.19
  252.1 16.1 %copy-start.15 = (bf16[8,32,8,128]{3,2,1,0:T(8,128)(2,1)S(1)}, bf16[8,32,8,128]{3,2,1,0:T(8,128)(2,1)}, u32[]{:S(2)}) copy-start(bf16[8,32,8,128]{3,2,1,0:T(8,128)(2,1)} %copy.136) | copy-start | bytes 1572868
  252.2 16.1 %copy-start.21 = (bf16[1,8,32,2048]{3,2,1,0:T(8,128)(2,1)S(1)}, bf16[1,8,32,2048]{3,2,1,0:T(8,128)(2,1)}, u32[]{:S(2)}) copy-start(bf16[1,8,32,2048]{3,2,1,0:T(8,128)(2,1)} %param.8) | copy-start | bytes 3145732
  286.2 115.6 %all-to-all-start.1 = ((bf16[8,3,32,2048]{3,2,1,0:T(8,128)(2,1)}), bf16[8,3,32,2048]{3,2,1,0:T(8,128)(2,1)}, u32[]{:S(2)}, u32[]{:S(2)}) async-start(bf16[8,3,32,2048]{3,2,1,0:T(8,128)(2,1)} %pad_maximum_fusion.1), calls=%async_computation.1 | async-start | bytes 6291456 | tf_op jit(solution)/shard_map/all_to_all | solution.py:197
  309.3 213.9 %reduce-scatter.9.cloned.1.call-start = ((), (), s32[]{:S(2)}) async-start(), calls=%async_computation.8 | async-start | bytes 4718592 | tf_op jit(solution)/shard_map/reduce_scatter | solution.py:229
  325.9 23.2 %collective-permute-start.1 = (bf16[4,32,2048]{2,0,1:T(4,128)(2,1)S(1)}, bf16[4,32,2048]{2,0,1:T(4,128)(2,1)S(1)}, u32[]{:S(2)}, u32[]{:S(2)}) collective-permute-start(bf16[4,32,2048]{2,0,1:T(4,128)(2,1)S(1)} %pad_maximum_fusion.5), channel_id=1, source_target_pairs={{4,0},{8,4},{12,8},{16,12},{20,16},{24,20},{28,24},{5,1},{9,5},{13... | collective-permute-start | bytes 1572872 | tf_op jit(solution)/shard_map/ppermute | solution.py:23
  405.8 5.2 copy-start.24
  405.8 5.2 copy-start.26
  411.0 3.2 copy-start.9
  416.3 3.3 copy-start.17
  419.6 195.5 %reduce-scatter.7.cloned.1.call-start = ((), (), s32[]{:S(2)}) async-start(), calls=%async_computation.7 | async-start | bytes 4718592 | tf_op jit(solution)/shard_map/reduce_scatter | solution.py:228
  423.2 5.6 copy-start.14
  423.2 215.7 %all-gather.4.cloned.1.call-start = ((), (), s32[]{:S(2)}) async-start(), calls=%async_computation.10 | async-start | bytes 2621440 | tf_op jit(solution)/shard_map/all_gather | solution.py:15
  423.8 260.4 %all-reduce.14.cloned.1.call-start = ((), (), s32[]{:S(2)}) async-start(), calls=%async_computation.11 | async-start | bytes 3145728 | tf_op jit(solution)/shard_map/psum | solution.py:234
  424.2 4.6 copy-start.28
  615.0 4.3 copy-start.29
  (8 other events, 14.6 us)
Sparse Core Ops, SparseCore 0:
  168.1 106.9 reduce-scatter.4
  278.7 152.0 reduce-scatter.10
  434.5 88.6 reduce-scatter.8
  526.6 88.3 reduce-scatter.6
  616.4 22.4 all-gather.3
  641.3 42.8 all-reduce.13
